TPU v7x, 32 devices: a whole 2x2x4 slice. The times are simulated.
32 devices in a mesh: group: 4 (over y, core), shard: 8 (over z, x).
Axes of the slice: x: 2, y: 2, z: 4, core: 2. Of those that a mesh axis runs over, the one named last changes fastest.
Arguments:
- queries: bfloat16 [512, 32, 128], P(('group', 'shard')), may hold values from -12 to 12
- passages: bfloat16 [2048, 64, 128], P(('group', 'shard')), may hold values from -4 to 4
- candidates: int32 [512, 160], P(('group', 'shard')), may hold values from 0 to 2047, as said below
- passage_slot: int32 [2048], replicated, may hold values from 0 to 2047, as said below
Outputs:
- scores: float32 [512, 160], P(('group', 'shard'))
Inputs may be any that keep to these rules, and one draw needn't show every extreme that they name: `passage_slot`: every storage row is named by exactly one passage id. `candidates`: candidates k * 20 to (k + 1) * 20 - 1 of a query, for k < 8, all lie in the storage rows of one device, rows d * 64 to (d + 1) * 64 - 1 of device d counted group-major. Over the 16 queries of one device, at most 12 such groups name any one device, and some devices are named exactly 12 times by the queries of every device.
All inputs are finite; a program needn't handle non-finite values.
Results may differ from a plain program's by a relative error of at most 0.0003.
Values may be sent and summed in bfloat16 or wider, within the bound.
No kernel may reach another device: no remote copies, remote signals or barrier semaphores. Data moves between devices by JAX's collectives and lax.ppermute only.
A program may use at most 64 MiB of HBM per device.

v0:
```python
import jax
import jax.numpy as jnp
from jax import lax
from jax.sharding import PartitionSpec as P

PER_VISIT = 20


def score_visits(query_rows, local_rows, passages):
    item_count, peer_width, qtok_count, dim_count = query_rows.shape
    slot_count, ptok_count = (passages.shape[0], passages.shape[1])
    visit_total = item_count * peer_width
    block_size = 16
    store_flat = passages.reshape(slot_count * ptok_count, dim_count)
    query_blocks = query_rows.reshape(visit_total // block_size, block_size, qtok_count, dim_count)
    row_blocks = local_rows.reshape(visit_total // block_size, block_size, local_rows.shape[2])
    slot_ids = jnp.arange(slot_count, dtype=jnp.int32)

    def one_block(pieces):
        query_block, row_block = pieces
        similarity = jnp.einsum(
            "vqd,sd->vqs", query_block, store_flat, preferred_element_type=jnp.float32
        )
        best_match = jnp.max(
            similarity.reshape(block_size, qtok_count, slot_count, ptok_count), axis=3
        )
        passage_score = jnp.sum(best_match, axis=1) / qtok_count
        picker = (row_block[:, :, None] == slot_ids[None, None, :]).astype(jnp.float32)
        return jnp.sum(picker * passage_score[:, None, :], axis=2)

    visit_scores = lax.map(one_block, (query_blocks, row_blocks))
    visit_scores = visit_scores.reshape(item_count, peer_width, local_rows.shape[2])
    return lax.all_to_all(visit_scores, ("group", "shard"), split_axis=1, concat_axis=1, tiled=True)


def local(queries, passages, candidates, passage_slot):
    peer_count = lax.axis_size(("group", "shard"))
    query_count, cand_count = candidates.shape
    slot_count = passages.shape[0]
    spread_count = cand_count // PER_VISIT
    capacity = 3 * query_count * spread_count // peer_count
    visit_count = query_count * spread_count
    storage = passage_slot[candidates].reshape(visit_count, PER_VISIT)
    target = storage[:, 0] // slot_count
    local_rows = storage % slot_count
    matches = (target[:, None] == jnp.arange(peer_count, dtype=jnp.int32)[None, :]).astype(
        jnp.int32
    )
    before = jnp.cumsum(matches, axis=0) - matches
    rank_in = jnp.sum(before * matches, axis=1)
    position = rank_in * peer_count + target
    holder = (
        jnp.zeros((capacity * peer_count,), jnp.int32)
        .at[position]
        .set(jnp.arange(visit_count, dtype=jnp.int32))
    )
    send_local = local_rows[holder].reshape(capacity, peer_count, PER_VISIT)
    query_local = holder // spread_count
    everyone = lax.all_gather(queries, ("group", "shard"), axis=0, tiled=True)
    query_global = (lax.axis_index(("group", "shard")) * query_count + query_local).reshape(
        capacity, peer_count
    )
    wanted = lax.all_to_all(
        query_global, ("group", "shard"), split_axis=1, concat_axis=1, tiled=True
    )
    local_block = lax.all_to_all(
        send_local, ("group", "shard"), split_axis=1, concat_axis=1, tiled=True
    )
    returned = score_visits(everyone[wanted], local_block, passages)
    flat_scores = returned.reshape(capacity * peer_count, PER_VISIT)[position]
    return flat_scores.reshape(query_count, cand_count)


def solution(mesh):
    return jax.shard_map(
        local,
        mesh=mesh,
        in_specs=(
            P(("group", "shard"), None, None),
            P(("group", "shard"), None, None),
            P(("group", "shard"), None),
            P(),
        ),
        out_specs=P(("group", "shard"), None),
        check_vma=False,
    )
```

profile of v0, /device:TPU:0, one launch (start us, length us, event | category | flops | bytes accessed | tf_op | source)
XLA Modules:
  0.0 248.6 jit_solution(6655536599872342939)
XLA Ops:
  6.5 0.7 all-gather.2.cloned.1.call-update
  7.3 0.7 compare_select_fusion.2
  8.1 13.6 %gather_fusion = s32[2560]{0:T(1024)S(1)} fusion(s32[2048]{0:T(1024)S(1)} %copy-done, s32[3072]{0:T(1024)S(1)} %pad_clamp_fusion), kind=kCustom, calls=%fused_computation | custom fusion | bytes 30720 | tf_op jit(solution)/shard_map/gather | solution.py:43
  22.7 1.0 scatter_custom_fusion
  23.7 0.7 copy.19
  24.4 7.3 %all-to-all-start.1 = ((s32[12,32,1]{0,2,1:T(1,128)}), s32[12,32,1]{0,2,1:T(1,128)S(1)}, u32[]{:S(2)}, u32[]{:S(2)}) async-start(s32[12,32,1]{0,2,1:T(1,128)} %copy.19), calls=%async_computation.1 | async-start | bytes 32768 | tf_op jit(solution)/shard_map/all_to_all | solution.py:63
  31.8 1.1 gather_fusion.1
  33.1 0.8 reshape.105
  33.9 5.0 %all-to-all-done.1 = s32[12,32,1]{0,2,1:T(1,128)S(1)} async-done(((s32[12,32,1]{0,2,1:T(1,128)}), s32[12,32,1]{0,2,1:T(1,128)S(1)}, u32[]{:S(2)}, u32[]{:S(2)}) %all-to-all-start.1) | async-done | bytes 1568 | tf_op jit(solution)/shard_map/all_to_all | solution.py:63
  38.8 2.5 %all-to-all-start = ((s32[32,1,240]{2,1,0:T(1,128)}), s32[32,1,240]{2,1,0:T(1,128)S(1)}, u32[]{:S(2)}, u32[]{:S(2)}) async-start(s32[32,1,240]{2,1,0:T(1,128)} %reshape.105), calls=%async_computation | async-start | bytes 65536 | tf_op jit(solution)/shard_map/all_to_all | solution.py:66
  41.6 7.0 %all-to-all-done = s32[32,1,240]{2,1,0:T(1,128)S(1)} async-done(((s32[32,1,240]{2,1,0:T(1,128)}), s32[32,1,240]{2,1,0:T(1,128)S(1)}, u32[]{:S(2)}, u32[]{:S(2)}) %all-to-all-start) | async-done | bytes 30752 | tf_op jit(solution)/shard_map/all_to_all | solution.py:66
  48.6 0.5 broadcast.107
  49.1 0.7 reduce.4
  50.1 24.7 %all-gather.2.cloned.1.call-done = bf16[512,32,128]{2,1,0:T(8,128)(2,1)} async-done(((bf16[16,32,128]{2,1,0:T(8,128)(2,1)}), bf16[512,32,128]{2,1,0:T(8,128)(2,1)}) %all-gather.2.cloned.1.call-update) | async-done | bytes 4194320 | tf_op jit(solution)/shard_map/all_gather | solution.py:59
  74.8 4.9 %gather_fusion.2 = bf16[384,32,128]{2,1,0:T(8,128)(2,1)} fusion(bf16[512,32,128]{2,1,0:T(8,128)(2,1)} %all-gather.2.cloned.1.call-done, s32[1024]{0:T(1024)S(1)} %pad_clamp_fusion.2), kind=kCustom, calls=%fused_computation.2 | custom fusion | bytes 6292992 | tf_op jit(solution)/shard_map/gather | solution.py:69
  79.7 147.7 %while.11 = (s32[]{:T(128)}, f32[24,16,20]{2,1,0:T(8,128)S(1)}, s32[24,16,20]{2,1,0:T(8,128)S(1)}, bf16[24,16,32,128]{3,2,1,0:T(8,128)(2,1)}, bf16[4096,128]{1,0:T(8,128)(2,1)S(1)}, /*index=5*/s32[]{:T(128)}, f32[]{:T(128)}) while((s32[]{:T(128)}, f32[24,16,20]{2,1,0:T(8,128)S(1)}, s32[24,16,20]{2,1,0:T(8,128)S(1)}, ...), condition=%wide.region_7.8_spmd.clone, body=%wide.region_3.7_spmd.clone.sunk | while | flops 539029184 | bytes 1484901 | solution.py:31
  79.8 5.5 %convolution_reduce_fusion.2 = f32[16,32,64]{1,2,0:T(8,128)S(1)} fusion(bf16[64,64,128,1]{2,1,0,3:T(8,128)(2,1)S(1)} %bitcast.53, bf16[24,16,32,128]{3,2,1,0:T(8,128)(2,1)} %get-tuple-element.110, s32[]{:T(128)S(6)} %copy.35), kind=kOutput, calls=%fused_computation.6.clone.1 | convolution fusion | flops 538935296 | bytes 1310724 | tf_op jit(solution)/shard_map/while/body/eval_jaxpr/vqd,sd->vqs/dot_general | solution.py:21
  85.4 0.2 reduce_sum.35
  86.0 5.5 %convolution_reduce_fusion.2 = f32[16,32,64]{1,2,0:T(8,128)S(1)} fusion(bf16[64,64,128,1]{2,1,0,3:T(8,128)(2,1)S(1)} %bitcast.53, bf16[24,16,32,128]{3,2,1,0:T(8,128)(2,1)} %get-tuple-element.110, s32[]{:T(128)S(6)} %copy.35), kind=kOutput, calls=%fused_computation.6.clone.1 | convolution fusion | flops 538935296 | bytes 1310724 | tf_op jit(solution)/shard_map/while/body/eval_jaxpr/vqd,sd->vqs/dot_general | solution.py:21
  92.1 5.5 %convolution_reduce_fusion.2 = f32[16,32,64]{1,2,0:T(8,128)S(1)} fusion(bf16[64,64,128,1]{2,1,0,3:T(8,128)(2,1)S(1)} %bitcast.53, bf16[24,16,32,128]{3,2,1,0:T(8,128)(2,1)} %get-tuple-element.110, s32[]{:T(128)S(6)} %copy.35), kind=kOutput, calls=%fused_computation.6.clone.1 | convolution fusion | flops 538935296 | bytes 1310724 | tf_op jit(solution)/shard_map/while/body/eval_jaxpr/vqd,sd->vqs/dot_general | solution.py:21
  98.3 5.5 %convolution_reduce_fusion.2 = f32[16,32,64]{1,2,0:T(8,128)S(1)} fusion(bf16[64,64,128,1]{2,1,0,3:T(8,128)(2,1)S(1)} %bitcast.53, bf16[24,16,32,128]{3,2,1,0:T(8,128)(2,1)} %get-tuple-element.110, s32[]{:T(128)S(6)} %copy.35), kind=kOutput, calls=%fused_computation.6.clone.1 | convolution fusion | flops 538935296 | bytes 1310724 | tf_op jit(solution)/shard_map/while/body/eval_jaxpr/vqd,sd->vqs/dot_general | solution.py:21
  104.5 5.5 %convolution_reduce_fusion.2 = f32[16,32,64]{1,2,0:T(8,128)S(1)} fusion(bf16[64,64,128,1]{2,1,0,3:T(8,128)(2,1)S(1)} %bitcast.53, bf16[24,16,32,128]{3,2,1,0:T(8,128)(2,1)} %get-tuple-element.110, s32[]{:T(128)S(6)} %copy.35), kind=kOutput, calls=%fused_computation.6.clone.1 | convolution fusion | flops 538935296 | bytes 1310724 | tf_op jit(solution)/shard_map/while/body/eval_jaxpr/vqd,sd->vqs/dot_general | solution.py:21
  110.6 5.5 %convolution_reduce_fusion.2 = f32[16,32,64]{1,2,0:T(8,128)S(1)} fusion(bf16[64,64,128,1]{2,1,0,3:T(8,128)(2,1)S(1)} %bitcast.53, bf16[24,16,32,128]{3,2,1,0:T(8,128)(2,1)} %get-tuple-element.110, s32[]{:T(128)S(6)} %copy.35), kind=kOutput, calls=%fused_computation.6.clone.1 | convolution fusion | flops 538935296 | bytes 1310724 | tf_op jit(solution)/shard_map/while/body/eval_jaxpr/vqd,sd->vqs/dot_general | solution.py:21
  116.8 5.5 %convolution_reduce_fusion.2 = f32[16,32,64]{1,2,0:T(8,128)S(1)} fusion(bf16[64,64,128,1]{2,1,0,3:T(8,128)(2,1)S(1)} %bitcast.53, bf16[24,16,32,128]{3,2,1,0:T(8,128)(2,1)} %get-tuple-element.110, s32[]{:T(128)S(6)} %copy.35), kind=kOutput, calls=%fused_computation.6.clone.1 | convolution fusion | flops 538935296 | bytes 1310724 | tf_op jit(solution)/shard_map/while/body/eval_jaxpr/vqd,sd->vqs/dot_general | solution.py:21
  122.9 5.5 %convolution_reduce_fusion.2 = f32[16,32,64]{1,2,0:T(8,128)S(1)} fusion(bf16[64,64,128,1]{2,1,0,3:T(8,128)(2,1)S(1)} %bitcast.53, bf16[24,16,32,128]{3,2,1,0:T(8,128)(2,1)} %get-tuple-element.110, s32[]{:T(128)S(6)} %copy.35), kind=kOutput, calls=%fused_computation.6.clone.1 | convolution fusion | flops 538935296 | bytes 1310724 | tf_op jit(solution)/shard_map/while/body/eval_jaxpr/vqd,sd->vqs/dot_general | solution.py:21
  129.1 5.5 %convolution_reduce_fusion.2 = f32[16,32,64]{1,2,0:T(8,128)S(1)} fusion(bf16[64,64,128,1]{2,1,0,3:T(8,128)(2,1)S(1)} %bitcast.53, bf16[24,16,32,128]{3,2,1,0:T(8,128)(2,1)} %get-tuple-element.110, s32[]{:T(128)S(6)} %copy.35), kind=kOutput, calls=%fused_computation.6.clone.1 | convolution fusion | flops 538935296 | bytes 1310724 | tf_op jit(solution)/shard_map/while/body/eval_jaxpr/vqd,sd->vqs/dot_general | solution.py:21
  135.2 5.5 %convolution_reduce_fusion.2 = f32[16,32,64]{1,2,0:T(8,128)S(1)} fusion(bf16[64,64,128,1]{2,1,0,3:T(8,128)(2,1)S(1)} %bitcast.53, bf16[24,16,32,128]{3,2,1,0:T(8,128)(2,1)} %get-tuple-element.110, s32[]{:T(128)S(6)} %copy.35), kind=kOutput, calls=%fused_computation.6.clone.1 | convolution fusion | flops 538935296 | bytes 1310724 | tf_op jit(solution)/shard_map/while/body/eval_jaxpr/vqd,sd->vqs/dot_general | solution.py:21
  141.4 5.5 %convolution_reduce_fusion.2 = f32[16,32,64]{1,2,0:T(8,128)S(1)} fusion(bf16[64,64,128,1]{2,1,0,3:T(8,128)(2,1)S(1)} %bitcast.53, bf16[24,16,32,128]{3,2,1,0:T(8,128)(2,1)} %get-tuple-element.110, s32[]{:T(128)S(6)} %copy.35), kind=kOutput, calls=%fused_computation.6.clone.1 | convolution fusion | flops 538935296 | bytes 1310724 | tf_op jit(solution)/shard_map/while/body/eval_jaxpr/vqd,sd->vqs/dot_general | solution.py:21
  147.5 5.5 %convolution_reduce_fusion.2 = f32[16,32,64]{1,2,0:T(8,128)S(1)} fusion(bf16[64,64,128,1]{2,1,0,3:T(8,128)(2,1)S(1)} %bitcast.53, bf16[24,16,32,128]{3,2,1,0:T(8,128)(2,1)} %get-tuple-element.110, s32[]{:T(128)S(6)} %copy.35), kind=kOutput, calls=%fused_computation.6.clone.1 | convolution fusion | flops 538935296 | bytes 1310724 | tf_op jit(solution)/shard_map/while/body/eval_jaxpr/vqd,sd->vqs/dot_general | solution.py:21
  153.7 5.5 %convolution_reduce_fusion.2 = f32[16,32,64]{1,2,0:T(8,128)S(1)} fusion(bf16[64,64,128,1]{2,1,0,3:T(8,128)(2,1)S(1)} %bitcast.53, bf16[24,16,32,128]{3,2,1,0:T(8,128)(2,1)} %get-tuple-element.110, s32[]{:T(128)S(6)} %copy.35), kind=kOutput, calls=%fused_computation.6.clone.1 | convolution fusion | flops 538935296 | bytes 1310724 | tf_op jit(solution)/shard_map/while/body/eval_jaxpr/vqd,sd->vqs/dot_general | solution.py:21
  159.9 5.5 %convolution_reduce_fusion.2 = f32[16,32,64]{1,2,0:T(8,128)S(1)} fusion(bf16[64,64,128,1]{2,1,0,3:T(8,128)(2,1)S(1)} %bitcast.53, bf16[24,16,32,128]{3,2,1,0:T(8,128)(2,1)} %get-tuple-element.110, s32[]{:T(128)S(6)} %copy.35), kind=kOutput, calls=%fused_computation.6.clone.1 | convolution fusion | flops 538935296 | bytes 1310724 | tf_op jit(solution)/shard_map/while/body/eval_jaxpr/vqd,sd->vqs/dot_general | solution.py:21
  166.0 5.5 %convolution_reduce_fusion.2 = f32[16,32,64]{1,2,0:T(8,128)S(1)} fusion(bf16[64,64,128,1]{2,1,0,3:T(8,128)(2,1)S(1)} %bitcast.53, bf16[24,16,32,128]{3,2,1,0:T(8,128)(2,1)} %get-tuple-element.110, s32[]{:T(128)S(6)} %copy.35), kind=kOutput, calls=%fused_computation.6.clone.1 | convolution fusion | flops 538935296 | bytes 1310724 | tf_op jit(solution)/shard_map/while/body/eval_jaxpr/vqd,sd->vqs/dot_general | solution.py:21
  172.2 5.5 %convolution_reduce_fusion.2 = f32[16,32,64]{1,2,0:T(8,128)S(1)} fusion(bf16[64,64,128,1]{2,1,0,3:T(8,128)(2,1)S(1)} %bitcast.53, bf16[24,16,32,128]{3,2,1,0:T(8,128)(2,1)} %get-tuple-element.110, s32[]{:T(128)S(6)} %copy.35), kind=kOutput, calls=%fused_computation.6.clone.1 | convolution fusion | flops 538935296 | bytes 1310724 | tf_op jit(solution)/shard_map/while/body/eval_jaxpr/vqd,sd->vqs/dot_general | solution.py:21
  178.3 5.5 %convolution_reduce_fusion.2 = f32[16,32,64]{1,2,0:T(8,128)S(1)} fusion(bf16[64,64,128,1]{2,1,0,3:T(8,128)(2,1)S(1)} %bitcast.53, bf16[24,16,32,128]{3,2,1,0:T(8,128)(2,1)} %get-tuple-element.110, s32[]{:T(128)S(6)} %copy.35), kind=kOutput, calls=%fused_computation.6.clone.1 | convolution fusion | flops 538935296 | bytes 1310724 | tf_op jit(solution)/shard_map/while/body/eval_jaxpr/vqd,sd->vqs/dot_general | solution.py:21
  184.5 5.5 %convolution_reduce_fusion.2 = f32[16,32,64]{1,2,0:T(8,128)S(1)} fusion(bf16[64,64,128,1]{2,1,0,3:T(8,128)(2,1)S(1)} %bitcast.53, bf16[24,16,32,128]{3,2,1,0:T(8,128)(2,1)} %get-tuple-element.110, s32[]{:T(128)S(6)} %copy.35), kind=kOutput, calls=%fused_computation.6.clone.1 | convolution fusion | flops 538935296 | bytes 1310724 | tf_op jit(solution)/shard_map/while/body/eval_jaxpr/vqd,sd->vqs/dot_general | solution.py:21
  190.6 5.5 %convolution_reduce_fusion.2 = f32[16,32,64]{1,2,0:T(8,128)S(1)} fusion(bf16[64,64,128,1]{2,1,0,3:T(8,128)(2,1)S(1)} %bitcast.53, bf16[24,16,32,128]{3,2,1,0:T(8,128)(2,1)} %get-tuple-element.110, s32[]{:T(128)S(6)} %copy.35), kind=kOutput, calls=%fused_computation.6.clone.1 | convolution fusion | flops 538935296 | bytes 1310724 | tf_op jit(solution)/shard_map/while/body/eval_jaxpr/vqd,sd->vqs/dot_general | solution.py:21
  196.8 5.5 %convolution_reduce_fusion.2 = f32[16,32,64]{1,2,0:T(8,128)S(1)} fusion(bf16[64,64,128,1]{2,1,0,3:T(8,128)(2,1)S(1)} %bitcast.53, bf16[24,16,32,128]{3,2,1,0:T(8,128)(2,1)} %get-tuple-element.110, s32[]{:T(128)S(6)} %copy.35), kind=kOutput, calls=%fused_computation.6.clone.1 | convolution fusion | flops 538935296 | bytes 1310724 | tf_op jit(solution)/shard_map/while/body/eval_jaxpr/vqd,sd->vqs/dot_general | solution.py:21
  202.9 5.5 %convolution_reduce_fusion.2 = f32[16,32,64]{1,2,0:T(8,128)S(1)} fusion(bf16[64,64,128,1]{2,1,0,3:T(8,128)(2,1)S(1)} %bitcast.53, bf16[24,16,32,128]{3,2,1,0:T(8,128)(2,1)} %get-tuple-element.110, s32[]{:T(128)S(6)} %copy.35), kind=kOutput, calls=%fused_computation.6.clone.1 | convolution fusion | flops 538935296 | bytes 1310724 | tf_op jit(solution)/shard_map/while/body/eval_jaxpr/vqd,sd->vqs/dot_general | solution.py:21
  209.1 5.5 %convolution_reduce_fusion.2 = f32[16,32,64]{1,2,0:T(8,128)S(1)} fusion(bf16[64,64,128,1]{2,1,0,3:T(8,128)(2,1)S(1)} %bitcast.53, bf16[24,16,32,128]{3,2,1,0:T(8,128)(2,1)} %get-tuple-element.110, s32[]{:T(128)S(6)} %copy.35), kind=kOutput, calls=%fused_computation.6.clone.1 | convolution fusion | flops 538935296 | bytes 1310724 | tf_op jit(solution)/shard_map/while/body/eval_jaxpr/vqd,sd->vqs/dot_general | solution.py:21
  215.3 5.5 %convolution_reduce_fusion.2 = f32[16,32,64]{1,2,0:T(8,128)S(1)} fusion(bf16[64,64,128,1]{2,1,0,3:T(8,128)(2,1)S(1)} %bitcast.53, bf16[24,16,32,128]{3,2,1,0:T(8,128)(2,1)} %get-tuple-element.110, s32[]{:T(128)S(6)} %copy.35), kind=kOutput, calls=%fused_computation.6.clone.1 | convolution fusion | flops 538935296 | bytes 1310724 | tf_op jit(solution)/shard_map/while/body/eval_jaxpr/vqd,sd->vqs/dot_general | solution.py:21
  221.4 5.5 %convolution_reduce_fusion.2 = f32[16,32,64]{1,2,0:T(8,128)S(1)} fusion(bf16[64,64,128,1]{2,1,0,3:T(8,128)(2,1)S(1)} %bitcast.53, bf16[24,16,32,128]{3,2,1,0:T(8,128)(2,1)} %get-tuple-element.110, s32[]{:T(128)S(6)} %copy.35), kind=kOutput, calls=%fused_computation.6.clone.1 | convolution fusion | flops 538935296 | bytes 1310724 | tf_op jit(solution)/shard_map/while/body/eval_jaxpr/vqd,sd->vqs/dot_general | solution.py:21
  227.6 0.8 reshape.107
  228.4 3.4 %all-to-all-start.2 = ((f32[32,1,240]{2,1,0:T(1,128)}), f32[32,1,240]{2,1,0:T(1,128)S(1)}, u32[]{:S(2)}, u32[]{:S(2)}) async-start(f32[32,1,240]{2,1,0:T(1,128)} %reshape.107), calls=%async_computation.2 | async-start | bytes 65536 | tf_op jit(solution)/shard_map/all_to_all | solution.py:33
  231.8 7.2 %all-to-all-done.2 = f32[32,1,240]{2,1,0:T(1,128)S(1)} async-done(((f32[32,1,240]{2,1,0:T(1,128)}), f32[32,1,240]{2,1,0:T(1,128)S(1)}, u32[]{:S(2)}, u32[]{:S(2)}) %all-to-all-start.2) | async-done | bytes 30752 | tf_op jit(solution)/shard_map/all_to_all | solution.py:33
  239.0 0.5 broadcast.108
  239.5 0.7 reduce.5
  240.4 0.6 gather_fusion.3
  241.1 0.7 reshape.52
  (199 shorter events, 15.9 us)
Async XLA Ops:
  6.5 1.5 copy-start
  6.5 68.3 %all-gather.2.cloned.1.call-start = ((), (), s32[]{:S(2)}) async-start(), calls=%async_computation.3 | async-start | bytes 4325376 | tf_op jit(solution)/shard_map/all_gather | solution.py:59
  24.4 14.4 %all-to-all-start.1 = ((s32[12,32,1]{0,2,1:T(1,128)}), s32[12,32,1]{0,2,1:T(1,128)S(1)}, u32[]{:S(2)}, u32[]{:S(2)}) async-start(s32[12,32,1]{0,2,1:T(1,128)} %copy.19), calls=%async_computation.1 | async-start | bytes 32768 | tf_op jit(solution)/shard_map/all_to_all | solution.py:63
  38.8 9.8 %all-to-all-start = ((s32[32,1,240]{2,1,0:T(1,128)}), s32[32,1,240]{2,1,0:T(1,128)S(1)}, u32[]{:S(2)}, u32[]{:S(2)}) async-start(s32[32,1,240]{2,1,0:T(1,128)} %reshape.105), calls=%async_computation | async-start | bytes 65536 | tf_op jit(solution)/shard_map/all_to_all | solution.py:66
  50.1 29.7 %copy-start.1 = (bf16[64,64,128]{2,1,0:T(8,128)(2,1)S(1)}, bf16[64,64,128]{2,1,0:T(8,128)(2,1)}, u32[]{:S(2)}) copy-start(bf16[64,64,128]{2,1,0:T(8,128)(2,1)} %param.7) | copy-start | bytes 3145732
  228.4 10.6 %all-to-all-start.2 = ((f32[32,1,240]{2,1,0:T(1,128)}), f32[32,1,240]{2,1,0:T(1,128)S(1)}, u32[]{:S(2)}, u32[]{:S(2)}) async-start(f32[32,1,240]{2,1,0:T(1,128)} %reshape.107), calls=%async_computation.2 | async-start | bytes 65536 | tf_op jit(solution)/shard_map/all_to_all | solution.py:33
Sparse Core Ops, SparseCore 0:
  10.3 64.4 all-gather.1
where the time goes:
time: 249 us
  matrix products  133 us (53%)
  waiting for transfers between devices  44.6 us (18%)
  local copies, waits for them, and re-layouts  30.6 us (12%)
  between operations  13.6 us (5%)
  starting transfers between devices  13.3 us (5%)
  other arithmetic  12.9 us (5%)
    dot_general x24, matrix products, one_block(): jnp.einsum('vqd,sd->vqs', query_block, store_flat, preferred_element_type...  133 us
    all_gather x1, waiting for transfers between devices, local(): everyone = lax.all_gather(queries, ('group', 'shard'), axis=0, tiled=True)  24.7 us
    gather x1, local copies, waits for them, and re-layouts, local(): storage = passage_slot[candidates].reshape(visit_count, PER_VISIT)  13.6 us
    all_to_all x1, starting transfers between devices, local(): lax.all_to_all(query_global, ('group', 'shard'), split_axis=1, concat_axi...  7.33 us
    all_to_all x1, waiting for transfers between devices, score_visits(): lax.all_to_all(visit_scores, ('group', 'shard'), split_axis=1, concat_axi...  7.18 us
    all_to_all x1, waiting for transfers between devices, local(): lax.all_to_all(send_local, ('group', 'shard'), split_axis=1, concat_axis=...  7.04 us
    reduce_sum x24, other arithmetic, one_block(): passage_score = jnp.sum(best_match, axis=1) / qtok_count  5.03 us
    all_to_all x1, waiting for transfers between devices, local(): lax.all_to_all(query_global, ('group', 'shard'), split_axis=1, concat_axi...  4.98 us
  transfers between devices with their start and end apart: 4, of which 4 were waited for; matrix products, arithmetic and copies ran while one was open for 8% of the time, Pallas kernels for 0%

commit v1 on v0

--- a/solution.py
+++ b/solution.py
@@ -60,8 +60,14 @@
     query_global = (lax.axis_index(("group", "shard")) * query_count + query_local).reshape(
         capacity, peer_count
     )
-    wanted = lax.all_to_all(
-        query_global, ("group", "shard"), split_axis=1, concat_axis=1, tiled=True
+    wanted = jnp.concatenate(
+        lax.all_to_all(
+            jnp.stack(jnp.split(query_global, lax.axis_size(("group", "shard")), axis=1)),
+            ("group", "shard"),
+            0,
+            0,
+        ),
+        axis=1,
     )
     local_block = lax.all_to_all(
         send_local, ("group", "shard"), split_axis=1, concat_axis=1, tiled=True

time: 249 us -> 249 us (level)
  waiting for transfers between devices: 44.6 us -> 21.2 us
  local copies, waits for them, and re-layouts: 30.6 us -> 46.7 us
  blocking collectives: 0 us -> 10.4 us
  starting transfers between devices: 13.3 us -> 9.87 us
    all_gather x1, waiting for transfers between devices: 24.7 us -> 8.22 us  [local(): everyone = lax.all_gather(queries, ('group', 'shard'), axis=0, tiled=True)]
    unnamed x8 -> x39, local copies, waits for them, and re-layouts: 1.83 us -> 17.1 us
    all_to_all x0 -> x1, blocking collectives: none -> 10.4 us  [score_visits(): lax.all_to_all(visit_scores, ('group', 'shard'), split_axis=1, concat_axi...]
    all_to_all x2 -> x1, waiting for transfers between devices: 12.2 us -> 4.98 us  [local(): lax.all_to_all(jnp.stack(jnp.split(query_global, lax.axis_size(('group',...]
    all_to_all x2 -> x1, starting transfers between devices: 10.7 us -> 7.33 us  [local(): lax.all_to_all(jnp.stack(jnp.split(query_global, lax.axis_size(('group',...]
  transfers between devices with their start and end apart: 4 -> 3, of which waited for: 4 -> 3; matrix products, arithmetic and copies ran while one was open for 8% -> 15% of each run, Pallas kernels for 0% -> 0%
where the time goes in v1:
time: 249 us
  matrix products  133 us (53%)
  local copies, waits for them, and re-layouts  46.7 us (19%)
  waiting for transfers between devices  21.2 us (9%)
  between operations  13.6 us (5%)
  other arithmetic  12.9 us (5%)
  blocking collectives  10.4 us (4%)
  starting transfers between devices  9.87 us (4%)
    dot_general x24, matrix products, one_block(): jnp.einsum('vqd,sd->vqs', query_block, store_flat, preferred_element_type...  133 us
    unnamed x39, local copies, waits for them, and re-layouts  17.1 us
    gather x1, local copies, waits for them, and re-layouts, local(): storage = passage_slot[candidates].reshape(visit_count, PER_VISIT)  13.6 us
    all_to_all x1, blocking collectives, score_visits(): lax.all_to_all(visit_scores, ('group', 'shard'), split_axis=1, concat_axi...  10.4 us
    all_gather x1, waiting for transfers between devices, local(): everyone = lax.all_gather(queries, ('group', 'shard'), axis=0, tiled=True)  8.22 us
    all_to_all x1, starting transfers between devices, local(): lax.all_to_all(jnp.stack(jnp.split(query_global, lax.axis_size(('group',...  7.33 us
    all_to_all x1, waiting for transfers between devices, local(): lax.all_to_all(send_local, ('group', 'shard'), split_axis=1, concat_axis=...  7.25 us
    reduce_sum x24, other arithmetic, one_block(): passage_score = jnp.sum(best_match, axis=1) / qtok_count  5.03 us
  transfers between devices with their start and end apart: 3, of which 3 were waited for; matrix products, arithmetic and copies ran while one was open for 15% of the time, Pallas kernels for 0%

profile of v1, /device:TPU:0, one launch (start us, length us, event | category | flops | bytes accessed | tf_op | source)
XLA Modules:
  0.0 248.6 jit_solution(3510382068403330313)
XLA Ops:
  6.5 0.7 all-gather.2.cloned.1.call-update
  7.3 0.7 compare_select_fusion.2
  8.1 13.6 %gather_fusion = s32[2560]{0:T(1024)S(1)} fusion(s32[2048]{0:T(1024)S(1)} %copy-done, s32[3072]{0:T(1024)S(1)} %pad_clamp_fusion), kind=kCustom, calls=%fused_computation | custom fusion | bytes 30720 | tf_op jit(solution)/shard_map/gather | solution.py:43
  22.7 1.0 scatter_custom_fusion
  24.2 0.5 slice_reduce_fusion
  24.7 0.5 constant_dynamic-update-slice_fusion.31
  25.7 0.5 constant_dynamic-update-slice_fusion.29
  26.2 0.5 constant_dynamic-update-slice_fusion.28
  26.7 0.5 constant_dynamic-update-slice_fusion.27
  27.2 0.5 constant_dynamic-update-slice_fusion.26
  41.1 7.3 %all-to-all-start.1 = ((s32[32,12,1]{1,2,0:T(1,128)}), s32[32,12,1]{1,2,0:T(1,128)S(1)}, u32[]{:S(2)}, u32[]{:S(2)}) async-start(s32[32,12,1]{1,2,0:T(1,128)} %constant_dynamic-update-slice_fusion), calls=%async_computation.1 | async-start | bytes 32768 | tf_op jit(solution)/shard_map/all_to_all | solution.py:64
  48.5 1.1 gather_fusion.1
  49.7 0.8 reshape.142
  50.5 5.0 %all-to-all-done.1 = s32[32,12,1]{1,2,0:T(1,128)S(1)} async-done(((s32[32,12,1]{1,2,0:T(1,128)}), s32[32,12,1]{1,2,0:T(1,128)S(1)}, u32[]{:S(2)}, u32[]{:S(2)}) %all-to-all-start.1) | async-done | bytes 1568 | tf_op jit(solution)/shard_map/all_to_all | solution.py:64
  55.5 2.5 %all-to-all-start = ((s32[32,1,240]{2,1,0:T(1,128)}), s32[32,1,240]{2,1,0:T(1,128)S(1)}, u32[]{:S(2)}, u32[]{:S(2)}) async-start(s32[32,1,240]{2,1,0:T(1,128)} %reshape.142), calls=%async_computation | async-start | bytes 65536 | tf_op jit(solution)/shard_map/all_to_all | solution.py:72
  58.2 7.3 %all-to-all-done = s32[32,1,240]{2,1,0:T(1,128)S(1)} async-done(((s32[32,1,240]{2,1,0:T(1,128)}), s32[32,1,240]{2,1,0:T(1,128)S(1)}, u32[]{:S(2)}, u32[]{:S(2)}) %all-to-all-start) | async-done | bytes 30752 | tf_op jit(solution)/shard_map/all_to_all | solution.py:72
  66.0 0.7 reduce.68
  66.9 8.2 %all-gather.2.cloned.1.call-done = bf16[512,32,128]{2,1,0:T(8,128)(2,1)} async-done(((bf16[16,32,128]{2,1,0:T(8,128)(2,1)}), bf16[512,32,128]{2,1,0:T(8,128)(2,1)}) %all-gather.2.cloned.1.call-update) | async-done | bytes 4194320 | tf_op jit(solution)/shard_map/all_gather | solution.py:59
  75.2 4.9 %gather_fusion.2 = bf16[384,32,128]{2,1,0:T(8,128)(2,1)} fusion(bf16[512,32,128]{2,1,0:T(8,128)(2,1)} %all-gather.2.cloned.1.call-done, s32[1024]{0:T(1024)S(1)} %pad_clamp_fusion.2), kind=kCustom, calls=%fused_computation.2 | custom fusion | bytes 6292992 | tf_op jit(solution)/shard_map/gather | solution.py:75
  80.1 148.2 %while.11 = (s32[]{:T(128)}, f32[24,16,20]{2,1,0:T(8,128)S(1)}, s32[24,16,20]{2,1,0:T(8,128)S(1)}, bf16[24,16,32,128]{3,2,1,0:T(8,128)(2,1)}, bf16[4096,128]{1,0:T(8,128)(2,1)S(1)}, /*index=5*/s32[]{:T(128)}, f32[]{:T(128)}) while((s32[]{:T(128)}, f32[24,16,20]{2,1,0:T(8,128)S(1)}, s32[24,16,20]{2,1,0:T(8,128)S(1)}, ...), condition=%wide.region_7.8_spmd.clone, body=%wide.region_3.7_spmd.clone.sunk | while | flops 539029184 | bytes 1485401 | solution.py:31
  80.1 5.6 %convolution_reduce_fusion.2 = f32[16,32,64]{1,2,0:T(8,128)S(1)} fusion(bf16[64,64,128,1]{2,1,0,3:T(8,128)(2,1)S(1)} %bitcast.118, bf16[24,16,32,128]{3,2,1,0:T(8,128)(2,1)} %get-tuple-element.144, s32[]{:T(128)} %get-tuple-element.134), kind=kOutput, calls=%fused_computation.6.clone.1 | convolution fusion | flops 538935296 | bytes 1311232 | tf_op jit(solution)/shard_map/while/body/eval_jaxpr/vqd,sd->vqs/dot_general | solution.py:21
  86.3 5.6 %convolution_reduce_fusion.2 = f32[16,32,64]{1,2,0:T(8,128)S(1)} fusion(bf16[64,64,128,1]{2,1,0,3:T(8,128)(2,1)S(1)} %bitcast.118, bf16[24,16,32,128]{3,2,1,0:T(8,128)(2,1)} %get-tuple-element.144, s32[]{:T(128)} %get-tuple-element.134), kind=kOutput, calls=%fused_computation.6.clone.1 | convolution fusion | flops 538935296 | bytes 1311232 | tf_op jit(solution)/shard_map/while/body/eval_jaxpr/vqd,sd->vqs/dot_general | solution.py:21
  92.4 5.5 %convolution_reduce_fusion.2 = f32[16,32,64]{1,2,0:T(8,128)S(1)} fusion(bf16[64,64,128,1]{2,1,0,3:T(8,128)(2,1)S(1)} %bitcast.118, bf16[24,16,32,128]{3,2,1,0:T(8,128)(2,1)} %get-tuple-element.144, s32[]{:T(128)} %get-tuple-element.134), kind=kOutput, calls=%fused_computation.6.clone.1 | convolution fusion | flops 538935296 | bytes 1311232 | tf_op jit(solution)/shard_map/while/body/eval_jaxpr/vqd,sd->vqs/dot_general | solution.py:21
  98.6 5.5 %convolution_reduce_fusion.2 = f32[16,32,64]{1,2,0:T(8,128)S(1)} fusion(bf16[64,64,128,1]{2,1,0,3:T(8,128)(2,1)S(1)} %bitcast.118, bf16[24,16,32,128]{3,2,1,0:T(8,128)(2,1)} %get-tuple-element.144, s32[]{:T(128)} %get-tuple-element.134), kind=kOutput, calls=%fused_computation.6.clone.1 | convolution fusion | flops 538935296 | bytes 1311232 | tf_op jit(solution)/shard_map/while/body/eval_jaxpr/vqd,sd->vqs/dot_general | solution.py:21
  104.8 5.5 %convolution_reduce_fusion.2 = f32[16,32,64]{1,2,0:T(8,128)S(1)} fusion(bf16[64,64,128,1]{2,1,0,3:T(8,128)(2,1)S(1)} %bitcast.118, bf16[24,16,32,128]{3,2,1,0:T(8,128)(2,1)} %get-tuple-element.144, s32[]{:T(128)} %get-tuple-element.134), kind=kOutput, calls=%fused_computation.6.clone.1 | convolution fusion | flops 538935296 | bytes 1311232 | tf_op jit(solution)/shard_map/while/body/eval_jaxpr/vqd,sd->vqs/dot_general | solution.py:21
  111.0 5.5 %convolution_reduce_fusion.2 = f32[16,32,64]{1,2,0:T(8,128)S(1)} fusion(bf16[64,64,128,1]{2,1,0,3:T(8,128)(2,1)S(1)} %bitcast.118, bf16[24,16,32,128]{3,2,1,0:T(8,128)(2,1)} %get-tuple-element.144, s32[]{:T(128)} %get-tuple-element.134), kind=kOutput, calls=%fused_computation.6.clone.1 | convolution fusion | flops 538935296 | bytes 1311232 | tf_op jit(solution)/shard_map/while/body/eval_jaxpr/vqd,sd->vqs/dot_general | solution.py:21
  117.1 5.5 %convolution_reduce_fusion.2 = f32[16,32,64]{1,2,0:T(8,128)S(1)} fusion(bf16[64,64,128,1]{2,1,0,3:T(8,128)(2,1)S(1)} %bitcast.118, bf16[24,16,32,128]{3,2,1,0:T(8,128)(2,1)} %get-tuple-element.144, s32[]{:T(128)} %get-tuple-element.134), kind=kOutput, calls=%fused_computation.6.clone.1 | convolution fusion | flops 538935296 | bytes 1311232 | tf_op jit(solution)/shard_map/while/body/eval_jaxpr/vqd,sd->vqs/dot_general | solution.py:21
  123.3 5.5 %convolution_reduce_fusion.2 = f32[16,32,64]{1,2,0:T(8,128)S(1)} fusion(bf16[64,64,128,1]{2,1,0,3:T(8,128)(2,1)S(1)} %bitcast.118, bf16[24,16,32,128]{3,2,1,0:T(8,128)(2,1)} %get-tuple-element.144, s32[]{:T(128)} %get-tuple-element.134), kind=kOutput, calls=%fused_computation.6.clone.1 | convolution fusion | flops 538935296 | bytes 1311232 | tf_op jit(solution)/shard_map/while/body/eval_jaxpr/vqd,sd->vqs/dot_general | solution.py:21
  129.5 5.5 %convolution_reduce_fusion.2 = f32[16,32,64]{1,2,0:T(8,128)S(1)} fusion(bf16[64,64,128,1]{2,1,0,3:T(8,128)(2,1)S(1)} %bitcast.118, bf16[24,16,32,128]{3,2,1,0:T(8,128)(2,1)} %get-tuple-element.144, s32[]{:T(128)} %get-tuple-element.134), kind=kOutput, calls=%fused_computation.6.clone.1 | convolution fusion | flops 538935296 | bytes 1311232 | tf_op jit(solution)/shard_map/while/body/eval_jaxpr/vqd,sd->vqs/dot_general | solution.py:21
  135.7 5.5 %convolution_reduce_fusion.2 = f32[16,32,64]{1,2,0:T(8,128)S(1)} fusion(bf16[64,64,128,1]{2,1,0,3:T(8,128)(2,1)S(1)} %bitcast.118, bf16[24,16,32,128]{3,2,1,0:T(8,128)(2,1)} %get-tuple-element.144, s32[]{:T(128)} %get-tuple-element.134), kind=kOutput, calls=%fused_computation.6.clone.1 | convolution fusion | flops 538935296 | bytes 1311232 | tf_op jit(solution)/shard_map/while/body/eval_jaxpr/vqd,sd->vqs/dot_general | solution.py:21
  141.8 5.5 %convolution_reduce_fusion.2 = f32[16,32,64]{1,2,0:T(8,128)S(1)} fusion(bf16[64,64,128,1]{2,1,0,3:T(8,128)(2,1)S(1)} %bitcast.118, bf16[24,16,32,128]{3,2,1,0:T(8,128)(2,1)} %get-tuple-element.144, s32[]{:T(128)} %get-tuple-element.134), kind=kOutput, calls=%fused_computation.6.clone.1 | convolution fusion | flops 538935296 | bytes 1311232 | tf_op jit(solution)/shard_map/while/body/eval_jaxpr/vqd,sd->vqs/dot_general | solution.py:21
  148.0 5.5 %convolution_reduce_fusion.2 = f32[16,32,64]{1,2,0:T(8,128)S(1)} fusion(bf16[64,64,128,1]{2,1,0,3:T(8,128)(2,1)S(1)} %bitcast.118, bf16[24,16,32,128]{3,2,1,0:T(8,128)(2,1)} %get-tuple-element.144, s32[]{:T(128)} %get-tuple-element.134), kind=kOutput, calls=%fused_computation.6.clone.1 | convolution fusion | flops 538935296 | bytes 1311232 | tf_op jit(solution)/shard_map/while/body/eval_jaxpr/vqd,sd->vqs/dot_general | solution.py:21
  154.2 5.5 %convolution_reduce_fusion.2 = f32[16,32,64]{1,2,0:T(8,128)S(1)} fusion(bf16[64,64,128,1]{2,1,0,3:T(8,128)(2,1)S(1)} %bitcast.118, bf16[24,16,32,128]{3,2,1,0:T(8,128)(2,1)} %get-tuple-element.144, s32[]{:T(128)} %get-tuple-element.134), kind=kOutput, calls=%fused_computation.6.clone.1 | convolution fusion | flops 538935296 | bytes 1311232 | tf_op jit(solution)/shard_map/while/body/eval_jaxpr/vqd,sd->vqs/dot_general | solution.py:21
  160.3 5.5 %convolution_reduce_fusion.2 = f32[16,32,64]{1,2,0:T(8,128)S(1)} fusion(bf16[64,64,128,1]{2,1,0,3:T(8,128)(2,1)S(1)} %bitcast.118, bf16[24,16,32,128]{3,2,1,0:T(8,128)(2,1)} %get-tuple-element.144, s32[]{:T(128)} %get-tuple-element.134), kind=kOutput, calls=%fused_computation.6.clone.1 | convolution fusion | flops 538935296 | bytes 1311232 | tf_op jit(solution)/shard_map/while/body/eval_jaxpr/vqd,sd->vqs/dot_general | solution.py:21
  166.5 5.5 %convolution_reduce_fusion.2 = f32[16,32,64]{1,2,0:T(8,128)S(1)} fusion(bf16[64,64,128,1]{2,1,0,3:T(8,128)(2,1)S(1)} %bitcast.118, bf16[24,16,32,128]{3,2,1,0:T(8,128)(2,1)} %get-tuple-element.144, s32[]{:T(128)} %get-tuple-element.134), kind=kOutput, calls=%fused_computation.6.clone.1 | convolution fusion | flops 538935296 | bytes 1311232 | tf_op jit(solution)/shard_map/while/body/eval_jaxpr/vqd,sd->vqs/dot_general | solution.py:21
  172.7 5.5 %convolution_reduce_fusion.2 = f32[16,32,64]{1,2,0:T(8,128)S(1)} fusion(bf16[64,64,128,1]{2,1,0,3:T(8,128)(2,1)S(1)} %bitcast.118, bf16[24,16,32,128]{3,2,1,0:T(8,128)(2,1)} %get-tuple-element.144, s32[]{:T(128)} %get-tuple-element.134), kind=kOutput, calls=%fused_computation.6.clone.1 | convolution fusion | flops 538935296 | bytes 1311232 | tf_op jit(solution)/shard_map/while/body/eval_jaxpr/vqd,sd->vqs/dot_general | solution.py:21
  178.9 5.5 %convolution_reduce_fusion.2 = f32[16,32,64]{1,2,0:T(8,128)S(1)} fusion(bf16[64,64,128,1]{2,1,0,3:T(8,128)(2,1)S(1)} %bitcast.118, bf16[24,16,32,128]{3,2,1,0:T(8,128)(2,1)} %get-tuple-element.144, s32[]{:T(128)} %get-tuple-element.134), kind=kOutput, calls=%fused_computation.6.clone.1 | convolution fusion | flops 538935296 | bytes 1311232 | tf_op jit(solution)/shard_map/while/body/eval_jaxpr/vqd,sd->vqs/dot_general | solution.py:21
  185.0 5.5 %convolution_reduce_fusion.2 = f32[16,32,64]{1,2,0:T(8,128)S(1)} fusion(bf16[64,64,128,1]{2,1,0,3:T(8,128)(2,1)S(1)} %bitcast.118, bf16[24,16,32,128]{3,2,1,0:T(8,128)(2,1)} %get-tuple-element.144, s32[]{:T(128)} %get-tuple-element.134), kind=kOutput, calls=%fused_computation.6.clone.1 | convolution fusion | flops 538935296 | bytes 1311232 | tf_op jit(solution)/shard_map/while/body/eval_jaxpr/vqd,sd->vqs/dot_general | solution.py:21
  191.2 5.5 %convolution_reduce_fusion.2 = f32[16,32,64]{1,2,0:T(8,128)S(1)} fusion(bf16[64,64,128,1]{2,1,0,3:T(8,128)(2,1)S(1)} %bitcast.118, bf16[24,16,32,128]{3,2,1,0:T(8,128)(2,1)} %get-tuple-element.144, s32[]{:T(128)} %get-tuple-element.134), kind=kOutput, calls=%fused_computation.6.clone.1 | convolution fusion | flops 538935296 | bytes 1311232 | tf_op jit(solution)/shard_map/while/body/eval_jaxpr/vqd,sd->vqs/dot_general | solution.py:21
  197.4 5.5 %convolution_reduce_fusion.2 = f32[16,32,64]{1,2,0:T(8,128)S(1)} fusion(bf16[64,64,128,1]{2,1,0,3:T(8,128)(2,1)S(1)} %bitcast.118, bf16[24,16,32,128]{3,2,1,0:T(8,128)(2,1)} %get-tuple-element.144, s32[]{:T(128)} %get-tuple-element.134), kind=kOutput, calls=%fused_computation.6.clone.1 | convolution fusion | flops 538935296 | bytes 1311232 | tf_op jit(solution)/shard_map/while/body/eval_jaxpr/vqd,sd->vqs/dot_general | solution.py:21
  203.6 5.5 %convolution_reduce_fusion.2 = f32[16,32,64]{1,2,0:T(8,128)S(1)} fusion(bf16[64,64,128,1]{2,1,0,3:T(8,128)(2,1)S(1)} %bitcast.118, bf16[24,16,32,128]{3,2,1,0:T(8,128)(2,1)} %get-tuple-element.144, s32[]{:T(128)} %get-tuple-element.134), kind=kOutput, calls=%fused_computation.6.clone.1 | convolution fusion | flops 538935296 | bytes 1311232 | tf_op jit(solution)/shard_map/while/body/eval_jaxpr/vqd,sd->vqs/dot_general | solution.py:21
  209.7 5.5 %convolution_reduce_fusion.2 = f32[16,32,64]{1,2,0:T(8,128)S(1)} fusion(bf16[64,64,128,1]{2,1,0,3:T(8,128)(2,1)S(1)} %bitcast.118, bf16[24,16,32,128]{3,2,1,0:T(8,128)(2,1)} %get-tuple-element.144, s32[]{:T(128)} %get-tuple-element.134), kind=kOutput, calls=%fused_computation.6.clone.1 | convolution fusion | flops 538935296 | bytes 1311232 | tf_op jit(solution)/shard_map/while/body/eval_jaxpr/vqd,sd->vqs/dot_general | solution.py:21
  215.9 5.5 %convolution_reduce_fusion.2 = f32[16,32,64]{1,2,0:T(8,128)S(1)} fusion(bf16[64,64,128,1]{2,1,0,3:T(8,128)(2,1)S(1)} %bitcast.118, bf16[24,16,32,128]{3,2,1,0:T(8,128)(2,1)} %get-tuple-element.144, s32[]{:T(128)} %get-tuple-element.134), kind=kOutput, calls=%fused_computation.6.clone.1 | convolution fusion | flops 538935296 | bytes 1311232 | tf_op jit(solution)/shard_map/while/body/eval_jaxpr/vqd,sd->vqs/dot_general | solution.py:21
  222.1 5.5 %convolution_reduce_fusion.2 = f32[16,32,64]{1,2,0:T(8,128)S(1)} fusion(bf16[64,64,128,1]{2,1,0,3:T(8,128)(2,1)S(1)} %bitcast.118, bf16[24,16,32,128]{3,2,1,0:T(8,128)(2,1)} %get-tuple-element.144, s32[]{:T(128)} %get-tuple-element.134), kind=kOutput, calls=%fused_computation.6.clone.1 | convolution fusion | flops 538935296 | bytes 1311232 | tf_op jit(solution)/shard_map/while/body/eval_jaxpr/vqd,sd->vqs/dot_general | solution.py:21
  228.5 10.4 %all_to_all.15 = f32[32,1,240]{2,1,0:T(1,128)S(1)} all-to-all(f32[32,1,240]{2,1,0:T(1,128)S(1)} %reshape.144), channel_id=1, replica_groups=mesh['group'=4,'shard'=8] {'group','shard'}, dimensions={0} | all-to-all | bytes 61440 | tf_op jit(solution)/shard_map/all_to_all | solution.py:33
  239.4 0.7 reduce.69
  240.4 0.6 gather_fusion.3
  241.0 0.7 reshape.57
  (230 shorter events, 31.6 us)
Async XLA Ops:
  6.5 1.5 copy-start
  6.5 68.6 %all-gather.2.cloned.1.call-start = ((), (), s32[]{:S(2)}) async-start(), calls=%async_computation.3 | async-start | bytes 4325376 | tf_op jit(solution)/shard_map/all_gather | solution.py:59
  41.1 14.4 %all-to-all-start.1 = ((s32[32,12,1]{1,2,0:T(1,128)}), s32[32,12,1]{1,2,0:T(1,128)S(1)}, u32[]{:S(2)}, u32[]{:S(2)}) async-start(s32[32,12,1]{1,2,0:T(1,128)} %constant_dynamic-update-slice_fusion), calls=%async_computation.1 | async-start | bytes 32768 | tf_op jit(solution)/shard_map/all_to_all | solution.py:64
  55.5 10.0 %all-to-all-start = ((s32[32,1,240]{2,1,0:T(1,128)}), s32[32,1,240]{2,1,0:T(1,128)S(1)}, u32[]{:S(2)}, u32[]{:S(2)}) async-start(s32[32,1,240]{2,1,0:T(1,128)} %reshape.142), calls=%async_computation | async-start | bytes 65536 | tf_op jit(solution)/shard_map/all_to_all | solution.py:72
  66.9 13.2 %copy-start.1 = (bf16[64,64,128]{2,1,0:T(8,128)(2,1)S(1)}, bf16[64,64,128]{2,1,0:T(8,128)(2,1)}, u32[]{:S(2)}) copy-start(bf16[64,64,128]{2,1,0:T(8,128)(2,1)} %param.7) | copy-start | bytes 3145732
Sparse Core Ops, SparseCore 0:
  10.3 64.7 all-gather.1
